TPU v7x, 32 devices: a whole 2x2x4 slice. The times are simulated.
32 devices in a mesh: seq: 16 (over z, y, x), head: 2 (over core).
Axes of the slice: x: 2, y: 2, z: 4, core: 2. Of those that a mesh axis runs over, the one named last changes fastest.
Arguments:
- queries: bfloat16 [1024, 1024], P('seq', 'head'), may hold values from -9 to 9
- keys: bfloat16 [2, 32768, 128], P('head', 'seq'), may hold values from -9 to 9
- values: bfloat16 [2, 32768, 128], P('head', 'seq'), may hold values from -6 to 6
- mask: int32 [8, 256], P(None, 'seq'), may hold values from 0 to 1, as said below
- out_proj: bfloat16 [1024, 4096], P('head', 'seq'), may hold values from -0.1875 to 0.1875
Outputs:
- output: bfloat16 [1024, 4096], P('seq', 'head')
Inputs may be any that keep to these rules, and one draw needn't show every extreme that they name: `mask`: each entry is 0 or 1; the share of ones differs strongly between the cached positions of different seq shards.
All inputs are finite; a program needn't handle non-finite values.
Results may differ from a plain program's by a relative error of at most 0.0057.
Values may be sent and summed in bfloat16 or wider, within the bound.
No kernel may reach another device: no remote copies, remote signals or barrier semaphores. Data moves between devices by JAX's collectives and lax.ppermute only.
A program may use at most 64 MiB of HBM per device.

v0:
```python
import jax
import jax.numpy as jnp
from jax import lax
from jax.sharding import PartitionSpec as P

BLK = 128


def on_device(queries, keys, values, mask, out_proj):
    gathered = lax.all_gather(queries, "seq", axis=0, tiled=True)
    rows = gathered.shape[0]
    head_size = keys.shape[2]
    group = gathered.shape[1] // head_size
    cached = keys.shape[1]
    query_heads = gathered.reshape(rows, group, head_size)
    key_local = keys[0]
    value_local = values[0]
    block = min(512, cached)
    count = cached // block
    mask_cols = block // BLK
    scale = 1.0 / jnp.sqrt(jnp.float32(head_size))
    offset = jnp.log(jnp.float32(cached * lax.axis_size("seq")))

    def block_sum(query_part, index, mask_part):
        start = index * block
        key_block = lax.dynamic_slice_in_dim(key_local, start, block, 0)
        value_block = lax.dynamic_slice_in_dim(value_local, start, block, 0)
        live = jnp.repeat(jnp.repeat(mask_part, BLK, axis=0), BLK, axis=1) > 0
        score = (
            jnp.einsum("qgd,kd->gqk", query_part, key_block, preferred_element_type=jnp.float32)
            * scale
            - offset
        )
        weight = jnp.where(live[None], jax.nn.sigmoid(score), 0.0).astype(jnp.bfloat16)
        return jnp.einsum("gqk,kd->qgd", weight, value_block, preferred_element_type=jnp.float32)

    def step(index, total):
        mask_part = lax.dynamic_slice_in_dim(mask, index * mask_cols, mask_cols, 1)
        return total + block_sum(query_heads, index, mask_part)

    attended = lax.fori_loop(0, count, step, jnp.zeros((rows, group, head_size), jnp.float32))
    partial_value = attended.reshape(rows, group * head_size)
    own_rows = rows // lax.axis_size("seq")
    summed = lax.psum(partial_value, "seq")
    mine = lax.dynamic_slice_in_dim(summed, lax.axis_index("seq") * own_rows, own_rows, 0)
    attended_bf = mine.astype(jnp.bfloat16)
    terms = jnp.dot(
        attended_bf,
        lax.all_gather(out_proj, "seq", axis=1, tiled=True),
        preferred_element_type=jnp.float32,
    )
    return lax.psum_scatter(terms, "head", scatter_dimension=1, tiled=True).astype(jnp.bfloat16)


def solution(mesh):
    placed = (
        P("seq", "head"),
        P("head", "seq", None),
        P("head", "seq", None),
        P(None, "seq"),
        P("head", "seq"),
    )
    return jax.shard_map(
        on_device, mesh=mesh, in_specs=placed, out_specs=P("seq", "head"), check_vma=False
    )
```

profile of v0, /device:TPU:0, one launch (start us, length us, event | category | flops | bytes accessed | tf_op | source)
XLA Modules:
  0.0 243.8 jit_solution(16637837117871356497)
XLA Ops:
  6.5 0.7 all-gather.3.cloned.1.call-update
  7.3 0.7 all-gather.5.cloned.1.call-update
  8.1 1.2 copy.6
  9.3 58.6 %all-gather.3.cloned.1.call-done = bf16[1024,512]{1,0:T(8,128)(2,1)} async-done(((bf16[64,512]{1,0:T(8,128)(2,1)}), bf16[1024,512]{1,0:T(8,128)(2,1)}) %all-gather.3.cloned.1.call-update) | async-done | bytes 1048592 | tf_op jit(solution)/shard_map/all_gather | solution.py:10
  67.9 2.1 reshape.31
  70.1 37.7 %while.16 = (s32[]{:T(128)}, f32[1024,4,128]{0,2,1:T(8,128)S(1)}, bf16[2048,128]{0,1:T(8,128)(2,1)S(1)}, s32[8,16]{1,0:T(8,128)}, bf16[2048,128]{1,0:T(8,128)(2,...) while((s32[]{:T(128)}, f32[1024,4,128]{0,2,1:T(8,128)S(1)}, ...), condition=%wide.region_1.2_spmd.clone, body=%wide.region_0.1_spmd.clone.sunk | while | flops 1089470464 | bytes 7612318 | solution.py:41
  70.1 0.8 dynamic-slice_compare_fusion.2
  70.9 3.2 %broadcast_in_dim.79 = pred[1024,4,128]{2,1,0:T(4,128)(4,1)S(1)} broadcast(pred[1024,4]{1,0:T(8,128)(4,1)S(1)} %bitcast.40), dimensions={0,1} | broadcast | bytes 528384 | tf_op jit(solution)/shard_map/while/body/eval_jaxpr/broadcast_in_dim | solution.py:28
  74.3 5.1 %bitcast_add_fusion.2 = f32[1024,4,128]{0,2,1:T(8,128)S(1)} fusion(f32[1024,4,128]{0,2,1:T(8,128)S(1)} %get-tuple-element.243, pred[1024,512]{1,0:T(8,128)(4,1)S(1)} %bitcast.41, bf16[1024,4,128]{2,1,0:T(4,128)(2,1)} %get-tuple-element.259, pred[]{:T(512)S(6)} %compare.3, bf16[2048,128]{1,0:T(8,128)(2,1)} %get-tuple-element.258, s32[]{:T(128)S(6)} %select_n.50, ...), kind=kOutput, calls=%fused_computation.4.clone.1 | convolution fusion | flops 1089470464 | bytes 6030848 | tf_op jit(solution)/shard_map/while/body/eval_jaxpr/gqk,kd->qgd/dot_general | solution.py:35
  79.5 0.8 dynamic-slice_compare_fusion.2
  80.3 3.2 %broadcast_in_dim.79 = pred[1024,4,128]{2,1,0:T(4,128)(4,1)S(1)} broadcast(pred[1024,4]{1,0:T(8,128)(4,1)S(1)} %bitcast.40), dimensions={0,1} | broadcast | bytes 528384 | tf_op jit(solution)/shard_map/while/body/eval_jaxpr/broadcast_in_dim | solution.py:28
  83.5 0.3 copy.17
  83.8 5.2 %bitcast_add_fusion.2 = f32[1024,4,128]{0,2,1:T(8,128)S(1)} fusion(f32[1024,4,128]{0,2,1:T(8,128)S(1)} %get-tuple-element.243, pred[1024,512]{1,0:T(8,128)(4,1)S(1)} %bitcast.41, bf16[1024,4,128]{2,1,0:T(4,128)(2,1)} %get-tuple-element.259, pred[]{:T(512)S(6)} %compare.3, bf16[2048,128]{1,0:T(8,128)(2,1)} %get-tuple-element.258, s32[]{:T(128)S(6)} %select_n.50, ...), kind=kOutput, calls=%fused_computation.4.clone.1 | convolution fusion | flops 1089470464 | bytes 6030848 | tf_op jit(solution)/shard_map/while/body/eval_jaxpr/gqk,kd->qgd/dot_general | solution.py:35
  89.0 0.8 dynamic-slice_compare_fusion.2
  89.8 3.2 %broadcast_in_dim.79 = pred[1024,4,128]{2,1,0:T(4,128)(4,1)S(1)} broadcast(pred[1024,4]{1,0:T(8,128)(4,1)S(1)} %bitcast.40), dimensions={0,1} | broadcast | bytes 528384 | tf_op jit(solution)/shard_map/while/body/eval_jaxpr/broadcast_in_dim | solution.py:28
  93.2 5.1 %bitcast_add_fusion.2 = f32[1024,4,128]{0,2,1:T(8,128)S(1)} fusion(f32[1024,4,128]{0,2,1:T(8,128)S(1)} %get-tuple-element.243, pred[1024,512]{1,0:T(8,128)(4,1)S(1)} %bitcast.41, bf16[1024,4,128]{2,1,0:T(4,128)(2,1)} %get-tuple-element.259, pred[]{:T(512)S(6)} %compare.3, bf16[2048,128]{1,0:T(8,128)(2,1)} %get-tuple-element.258, s32[]{:T(128)S(6)} %select_n.50, ...), kind=kOutput, calls=%fused_computation.4.clone.1 | convolution fusion | flops 1089470464 | bytes 6030848 | tf_op jit(solution)/shard_map/while/body/eval_jaxpr/gqk,kd->qgd/dot_general | solution.py:35
  98.4 0.8 dynamic-slice_compare_fusion.2
  99.2 3.2 %broadcast_in_dim.79 = pred[1024,4,128]{2,1,0:T(4,128)(4,1)S(1)} broadcast(pred[1024,4]{1,0:T(8,128)(4,1)S(1)} %bitcast.40), dimensions={0,1} | broadcast | bytes 528384 | tf_op jit(solution)/shard_map/while/body/eval_jaxpr/broadcast_in_dim | solution.py:28
  102.4 0.3 copy.17
  102.6 5.1 %bitcast_add_fusion.2 = f32[1024,4,128]{0,2,1:T(8,128)S(1)} fusion(f32[1024,4,128]{0,2,1:T(8,128)S(1)} %get-tuple-element.243, pred[1024,512]{1,0:T(8,128)(4,1)S(1)} %bitcast.41, bf16[1024,4,128]{2,1,0:T(4,128)(2,1)} %get-tuple-element.259, pred[]{:T(512)S(6)} %compare.3, bf16[2048,128]{1,0:T(8,128)(2,1)} %get-tuple-element.258, s32[]{:T(128)S(6)} %select_n.50, ...), kind=kOutput, calls=%fused_computation.4.clone.1 | convolution fusion | flops 1089470464 | bytes 6030848 | tf_op jit(solution)/shard_map/while/body/eval_jaxpr/gqk,kd->qgd/dot_general | solution.py:35
  107.8 116.3 %all-reduce.1 = bf16[1024,512]{0,1:T(8,128)(2,1)S(1)} all-reduce(f32[1024,512]{0,1:T(8,128)S(1)} %bitcast.42), channel_id=1, replica_groups=mesh['seq'=16,'head'=2] {'seq'}, use_global_device_ids=true, to_apply=%region_2.3 | all-reduce | flops 524288 | bytes 3145728 | tf_op jit(solution)/shard_map/psum | solution.py:44
  224.1 4.1 %fusion.21 = f32[64,4096]{1,0:T(8,128)} fusion(bf16[512,4096]{1,0:T(8,128)(2,1)} %all-gather.5.cloned.1.call-done, bf16[1024,512]{0,1:T(8,128)(2,1)S(1)} %all-reduce.1, s32[]{:T(128)S(6)} %select_n.35), kind=kOutput, calls=%fused_computation.18 | convolution fusion | flops 268435456 | bytes 5373956 | tf_op jit(solution)/shard_map/dot_general | solution.py:47
  228.3 7.3 %reduce-scatter.2.cloned.1.call-done = f32[64,2048]{1,0:T(8,128)} async-done(((f32[64,4096]{1,0:T(8,128)}), f32[64,2048]{1,0:T(8,128)}) %reduce-scatter.2.cloned.1.call-update) | async-done | bytes 524304 | tf_op jit(solution)/shard_map/reduce_scatter | solution.py:52
  235.5 1.8 convert_element_type.17
  (12 shorter events, 0.8 us)
Async XLA Ops:
  6.5 61.4 %all-gather.3.cloned.1.call-start = ((), (), s32[]{:S(2)}) async-start(), calls=%async_computation.1 | async-start | bytes 1114112 | tf_op jit(solution)/shard_map/all_gather | solution.py:10
  7.3 216.9 %all-gather.5.cloned.1.call-start = ((), (), s32[]{:S(2)}) async-start(), calls=%async_computation.2 | async-start | bytes 4456448 | tf_op jit(solution)/shard_map/all_gather | solution.py:49
  8.0 227.5 %reduce-scatter.2.cloned.1.call-start = ((), (), s32[]{:S(2)}) async-start(), calls=%async_computation.3 | async-start | bytes 1572864 | tf_op jit(solution)/shard_map/reduce_scatter | solution.py:52
Sparse Core Ops, SparseCore 0:
  10.1 57.7 all-gather.2
  70.7 100.2 all-gather.4
  228.4 7.0 reduce-scatter.1
where the time goes:
time: 244 us
  blocking collectives  116 us (48%)
  waiting for transfers between devices  67.3 us (28%)
  matrix products  24.7 us (10%)
  local copies, waits for them, and re-layouts  17.3 us (7%)
  between operations  13.2 us (5%)
  other arithmetic  4.83 us (2%)
    psum x1, blocking collectives, on_device(): summed = lax.psum(partial_value, 'seq')  116 us
    all_gather x1, waiting for transfers between devices, on_device(): gathered = lax.all_gather(queries, 'seq', axis=0, tiled=True)  58.6 us
    dot_general x4, matrix products, block_sum(): jnp.einsum('gqk,kd->qgd', weight, value_block, preferred_element_type=jnp...  20.6 us
    broadcast_in_dim x8, local copies, waits for them, and re-layouts, block_sum(): live = jnp.repeat(jnp.repeat(mask_part, BLK, axis=0), BLK, axis=1) > 0  12.9 us
    reduce_scatter x1, waiting for transfers between devices, on_device(): lax.psum_scatter(terms, 'head', scatter_dimension=1, tiled=True)  7.26 us
  transfers between devices with their start and end apart: 3, of which 2 were waited for; matrix products, arithmetic and copies ran while one was open for 17% of the time, Pallas kernels for 0%

commit v1 on v0

--- a/solution.py
+++ b/solution.py
@@ -6,8 +6,25 @@
 BLK = 128
 
 
+def laid_out(pieces, dim):
+    dims = list(pieces.shape[1:])
+    dims[dim] *= pieces.shape[0]
+    return jnp.moveaxis(pieces, 0, dim).reshape(dims)
+
+
+def doubled(x, axis):
+    length, here = (lax.axis_size(axis), lax.axis_index(axis))
+    pieces, bit = (x[None], 1)
+    while bit < length:
+        other = lax.ppermute(pieces, axis, [(i, i ^ bit) for i in range(length)])
+        low = here & bit == 0
+        pieces = jnp.concatenate([jnp.where(low, pieces, other), jnp.where(low, other, pieces)])
+        bit *= 2
+    return pieces
+
+
 def on_device(queries, keys, values, mask, out_proj):
-    gathered = lax.all_gather(queries, "seq", axis=0, tiled=True)
+    gathered = laid_out(doubled(queries, "seq"), 0)
     rows = gathered.shape[0]
     head_size = keys.shape[2]
     group = gathered.shape[1] // head_size

time: 244 us -> 218 us (0.89)
  waiting for transfers between devices: 67.3 us -> 38.2 us
  starting transfers between devices: 0.08 us -> 10.3 us
  blocking collectives: 116 us -> 109 us
    all_gather x1 -> x0, waiting for transfers between devices: 58.6 us -> none  [on_device(): gathered = lax.all_gather(queries, 'seq', axis=0, tiled=True)]
    ppermute x0 -> x4, waiting for transfers between devices: none -> 30.7 us  [doubled(): other = lax.ppermute(pieces, axis, [(i, i ^ bit) for i in range(length)])]
    ppermute x0 -> x4, starting transfers between devices: none -> 10.3 us  [doubled(): other = lax.ppermute(pieces, axis, [(i, i ^ bit) for i in range(length)])]
    psum x1, blocking collectives: 116 us -> 109 us  [on_device(): summed = lax.psum(partial_value, 'seq')]
    gt x4, other arithmetic: 3.06 us -> 0.31 us  [block_sum(): live = jnp.repeat(jnp.repeat(mask_part, BLK, axis=0), BLK, axis=1) > 0]
  transfers between devices with their start and end apart: 3 -> 6, of which waited for: 2 -> 5; matrix products, arithmetic and copies ran while one was open for 17% -> 18% of each run, Pallas kernels for 0% -> 0%
where the time goes in v1:
time: 218 us; the launch traced here: 217 us
  blocking collectives  109 us (50%)
  waiting for transfers between devices  38.2 us (18%)
  matrix products  25 us (11%)
  local copies, waits for them, and re-layouts  17.1 us (8%)
  between operations  13.5 us (6%)
  starting transfers between devices  10.3 us (5%)
  other arithmetic  4.05 us (2%)
    psum x1, blocking collectives, on_device(): summed = lax.psum(partial_value, 'seq')  109 us
    ppermute x4, waiting for transfers between devices, doubled(): other = lax.ppermute(pieces, axis, [(i, i ^ bit) for i in range(length)])  30.7 us
    dot_general x4, matrix products, block_sum(): jnp.einsum('gqk,kd->qgd', weight, value_block, preferred_element_type=jnp...  20.9 us
    broadcast_in_dim x8, local copies, waits for them, and re-layouts, block_sum(): live = jnp.repeat(jnp.repeat(mask_part, BLK, axis=0), BLK, axis=1) > 0  12.9 us
    ppermute x4, starting transfers between devices, doubled(): other = lax.ppermute(pieces, axis, [(i, i ^ bit) for i in range(length)])  10.3 us
    reduce_scatter x1, waiting for transfers between devices, on_device(): lax.psum_scatter(terms, 'head', scatter_dimension=1, tiled=True)  7.43 us
  transfers between devices with their start and end apart: 6, of which 5 were waited for; matrix products, arithmetic and copies ran while one was open for 18% of the time, Pallas kernels for 0%

profile of v1, /device:TPU:0, one launch (start us, length us, event | category | flops | bytes accessed | tf_op | source)
XLA Modules:
  0.0 217.5 jit_solution(5366662287644767438)
XLA Ops:
  6.5 3.0 %collective-permute-start = (bf16[1,64,512]{2,1,0:T(8,128)(2,1)}, bf16[1,64,512]{2,1,0:T(8,128)(2,1)S(1)}, u32[]{:S(2)}, u32[]{:S(2)}) collective-permute-start(bf16[1,64,512]{2,1,0:T(8,128)(2,1)} %bitcast.47), channel_id=1, source_target_pairs={{0,2},{2,0},{4,6},{6,4},{8,10},{10,8},{12,14},{14,12},{16,18},{18,... | collective-permute-start | bytes 196616 | tf_op jit(solution)/shard_map/ppermute | solution.py:19
  9.5 2.5 %collective-permute-done = bf16[1,64,512]{2,1,0:T(8,128)(2,1)S(1)} collective-permute-done((bf16[1,64,512]{2,1,0:T(8,128)(2,1)}, bf16[1,64,512]{2,1,0:T(8,128)(2,1)S(1)}, u32[]{:S(2)}, u32[]{:S(2)}) %collective-permute-start) | collective-permute-done | bytes 65568 | tf_op jit(solution)/shard_map/ppermute | solution.py:19
  12.0 0.9 broadcast_select_fusion.7
  12.8 2.1 collective-permute-start.1
  15.0 2.9 %collective-permute-done.1 = bf16[2,64,512]{2,1,0:T(8,128)(2,1)S(1)} collective-permute-done((bf16[2,64,512]{2,1,0:T(8,128)(2,1)S(1)}, bf16[2,64,512]{2,1,0:T(8,128)(2,1)S(1)}, u32[]{:S(2)}, u32[]{:S(2)}) %collective-permute-start.1) | collective-permute-done | bytes 131104 | tf_op jit(solution)/shard_map/ppermute | solution.py:19
  18.0 2.1 collective-permute-start.2
  20.1 4.4 %collective-permute-done.2 = bf16[4,64,512]{2,1,0:T(8,128)(2,1)S(1)} collective-permute-done((bf16[4,64,512]{2,1,0:T(8,128)(2,1)S(1)}, bf16[4,64,512]{2,1,0:T(8,128)(2,1)S(1)}, u32[]{:S(2)}, u32[]{:S(2)}) %collective-permute-start.2) | collective-permute-done | bytes 262176 | tf_op jit(solution)/shard_map/ppermute | solution.py:19
  25.4 3.0 %collective-permute-start.3 = (bf16[8,64,512]{2,1,0:T(8,128)(2,1)}, bf16[8,64,512]{2,1,0:T(8,128)(2,1)S(1)}, u32[]{:S(2)}, u32[]{:S(2)}) collective-permute-start(bf16[8,64,512]{2,1,0:T(8,128)(2,1)} %pad_maximum_fusion.1), channel_id=1, source_target_pairs={{0,16},{2,18},{4,20},{6,22},{8,24},{10,26},{12,28},{14,30},{16,0},... | collective-permute-start | bytes 1572872 | tf_op jit(solution)/shard_map/ppermute | solution.py:19
  28.5 2.1 copy.6
  30.6 20.9 %collective-permute-done.3 = bf16[8,64,512]{2,1,0:T(8,128)(2,1)S(1)} collective-permute-done((bf16[8,64,512]{2,1,0:T(8,128)(2,1)}, bf16[8,64,512]{2,1,0:T(8,128)(2,1)S(1)}, u32[]{:S(2)}, u32[]{:S(2)}) %collective-permute-start.3) | collective-permute-done | bytes 524320 | tf_op jit(solution)/shard_map/ppermute | solution.py:19
  51.7 1.1 reshape_reshape.3
  52.8 35.3 %while.16 = (s32[]{:T(128)}, f32[1024,4,128]{0,2,1:T(8,128)S(1)}, bf16[2048,128]{0,1:T(8,128)(2,1)}, s32[8,16]{1,0:T(8,128)S(1)}, bf16[2048,128]{1,0:T(8,128)(2,...) while((s32[]{:T(128)}, f32[1024,4,128]{0,2,1:T(8,128)S(1)}, ...), condition=%wide.region_1.2_spmd.clone, body=%wide.region_0.1_spmd.clone.sunk | while | flops 1089470464 | bytes 7612318 | solution.py:58
  52.9 3.2 %broadcast_in_dim.83 = pred[1024,4,128]{2,1,0:T(4,128)(4,1)S(1)} broadcast(pred[1024,4]{1,0:T(8,128)(4,1)S(1)} %bitcast.43), dimensions={0,1} | broadcast | bytes 528384 | tf_op jit(solution)/shard_map/while/body/eval_jaxpr/broadcast_in_dim | solution.py:45
  56.4 5.2 %bitcast_add_fusion.2 = f32[1024,4,128]{0,2,1:T(8,128)S(1)} fusion(f32[1024,4,128]{0,2,1:T(8,128)S(1)} %get-tuple-element.251, pred[1024,512]{1,0:T(8,128)(4,1)S(1)} %bitcast.44, bf16[1024,4,128]{2,1,0:T(4,128)(2,1)} %get-tuple-element.267, pred[]{:T(512)S(6)} %compare.3, bf16[2048,128]{1,0:T(8,128)(2,1)} %get-tuple-element.266, s32[]{:T(128)S(6)} %select_n.126, ...), kind=kOutput, calls=%fused_computation.4.clone.1 | convolution fusion | flops 1089470464 | bytes 6030848 | tf_op jit(solution)/shard_map/while/body/eval_jaxpr/gqk,kd->qgd/dot_general | solution.py:52
  61.7 3.2 %broadcast_in_dim.83 = pred[1024,4,128]{2,1,0:T(4,128)(4,1)S(1)} broadcast(pred[1024,4]{1,0:T(8,128)(4,1)S(1)} %bitcast.43), dimensions={0,1} | broadcast | bytes 528384 | tf_op jit(solution)/shard_map/while/body/eval_jaxpr/broadcast_in_dim | solution.py:45
  65.2 5.2 %bitcast_add_fusion.2 = f32[1024,4,128]{0,2,1:T(8,128)S(1)} fusion(f32[1024,4,128]{0,2,1:T(8,128)S(1)} %get-tuple-element.251, pred[1024,512]{1,0:T(8,128)(4,1)S(1)} %bitcast.44, bf16[1024,4,128]{2,1,0:T(4,128)(2,1)} %get-tuple-element.267, pred[]{:T(512)S(6)} %compare.3, bf16[2048,128]{1,0:T(8,128)(2,1)} %get-tuple-element.266, s32[]{:T(128)S(6)} %select_n.126, ...), kind=kOutput, calls=%fused_computation.4.clone.1 | convolution fusion | flops 1089470464 | bytes 6030848 | tf_op jit(solution)/shard_map/while/body/eval_jaxpr/gqk,kd->qgd/dot_general | solution.py:52
  70.5 3.2 %broadcast_in_dim.83 = pred[1024,4,128]{2,1,0:T(4,128)(4,1)S(1)} broadcast(pred[1024,4]{1,0:T(8,128)(4,1)S(1)} %bitcast.43), dimensions={0,1} | broadcast | bytes 528384 | tf_op jit(solution)/shard_map/while/body/eval_jaxpr/broadcast_in_dim | solution.py:45
  74.0 5.2 %bitcast_add_fusion.2 = f32[1024,4,128]{0,2,1:T(8,128)S(1)} fusion(f32[1024,4,128]{0,2,1:T(8,128)S(1)} %get-tuple-element.251, pred[1024,512]{1,0:T(8,128)(4,1)S(1)} %bitcast.44, bf16[1024,4,128]{2,1,0:T(4,128)(2,1)} %get-tuple-element.267, pred[]{:T(512)S(6)} %compare.3, bf16[2048,128]{1,0:T(8,128)(2,1)} %get-tuple-element.266, s32[]{:T(128)S(6)} %select_n.126, ...), kind=kOutput, calls=%fused_computation.4.clone.1 | convolution fusion | flops 1089470464 | bytes 6030848 | tf_op jit(solution)/shard_map/while/body/eval_jaxpr/gqk,kd->qgd/dot_general | solution.py:52
  79.3 3.2 %broadcast_in_dim.83 = pred[1024,4,128]{2,1,0:T(4,128)(4,1)S(1)} broadcast(pred[1024,4]{1,0:T(8,128)(4,1)S(1)} %bitcast.43), dimensions={0,1} | broadcast | bytes 528384 | tf_op jit(solution)/shard_map/while/body/eval_jaxpr/broadcast_in_dim | solution.py:45
  82.8 5.3 %bitcast_add_fusion.2 = f32[1024,4,128]{0,2,1:T(8,128)S(1)} fusion(f32[1024,4,128]{0,2,1:T(8,128)S(1)} %get-tuple-element.251, pred[1024,512]{1,0:T(8,128)(4,1)S(1)} %bitcast.44, bf16[1024,4,128]{2,1,0:T(4,128)(2,1)} %get-tuple-element.267, pred[]{:T(512)S(6)} %compare.3, bf16[2048,128]{1,0:T(8,128)(2,1)} %get-tuple-element.266, s32[]{:T(128)S(6)} %select_n.126, ...), kind=kOutput, calls=%fused_computation.4.clone.1 | convolution fusion | flops 1089470464 | bytes 6030848 | tf_op jit(solution)/shard_map/while/body/eval_jaxpr/gqk,kd->qgd/dot_general | solution.py:52
  88.1 109.2 %all-reduce.1 = bf16[1024,512]{0,1:T(8,128)(2,1)S(1)} all-reduce(f32[1024,512]{0,1:T(8,128)S(1)} %bitcast.45), channel_id=1, replica_groups=mesh['seq'=16,'head'=2] {'seq'}, use_global_device_ids=true, to_apply=%region_2.3 | all-reduce | flops 524288 | bytes 3145728 | tf_op jit(solution)/shard_map/psum | solution.py:61
  197.3 4.1 %fusion.21 = f32[64,4096]{1,0:T(8,128)} fusion(bf16[512,4096]{1,0:T(8,128)(2,1)} %all-gather.2.cloned.1.call-done, bf16[1024,512]{0,1:T(8,128)(2,1)S(1)} %all-reduce.1, s32[]{:T(128)S(6)} %select_n.95), kind=kOutput, calls=%fused_computation.25 | convolution fusion | flops 268435456 | bytes 5373956 | tf_op jit(solution)/shard_map/dot_general | solution.py:64
  201.4 7.4 %reduce-scatter.2.cloned.1.call-done = f32[64,2048]{1,0:T(8,128)} async-done(((f32[64,4096]{1,0:T(8,128)}), f32[64,2048]{1,0:T(8,128)}) %reduce-scatter.2.cloned.1.call-update) | async-done | bytes 524304 | tf_op jit(solution)/shard_map/reduce_scatter | solution.py:69
  208.9 1.8 convert_element_type.17
  (27 shorter events, 2.7 us)
Async XLA Ops:
  6.5 190.8 %all-gather.2.cloned.1.call-start = ((), (), s32[]{:S(2)}) async-start(), calls=%async_computation.1 | async-start | bytes 4456448 | tf_op jit(solution)/shard_map/all_gather | solution.py:66
  6.5 5.4 %collective-permute-start = (bf16[1,64,512]{2,1,0:T(8,128)(2,1)}, bf16[1,64,512]{2,1,0:T(8,128)(2,1)S(1)}, u32[]{:S(2)}, u32[]{:S(2)}) collective-permute-start(bf16[1,64,512]{2,1,0:T(8,128)(2,1)} %bitcast.47), channel_id=1, source_target_pairs={{0,2},{2,0},{4,6},{6,4},{8,10},{10,8},{12,14},{14,12},{16,18},{18,... | collective-permute-start | bytes 196616 | tf_op jit(solution)/shard_map/ppermute | solution.py:19
  12.8 5.1 %collective-permute-start.1 = (bf16[2,64,512]{2,1,0:T(8,128)(2,1)S(1)}, bf16[2,64,512]{2,1,0:T(8,128)(2,1)S(1)}, u32[]{:S(2)}, u32[]{:S(2)}) collective-permute-start(bf16[2,64,512]{2,1,0:T(8,128)(2,1)S(1)} %pad_maximum_fusion.3), channel_id=1, source_target_pairs={{0,4},{2,6},{4,0},{6,2},{8,12},{10,14},{12,8},{14,10},{16,20},{18,... | collective-permute-start | bytes 393224 | tf_op jit(solution)/shard_map/ppermute | solution.py:19
  18.0 6.5 %collective-permute-start.2 = (bf16[4,64,512]{2,1,0:T(8,128)(2,1)S(1)}, bf16[4,64,512]{2,1,0:T(8,128)(2,1)S(1)}, u32[]{:S(2)}, u32[]{:S(2)}) collective-permute-start(bf16[4,64,512]{2,1,0:T(8,128)(2,1)S(1)} %pad_maximum_fusion.2), channel_id=1, source_target_pairs={{0,8},{2,10},{4,12},{6,14},{8,0},{10,2},{12,4},{14,6},{16,24},{18,... | collective-permute-start | bytes 786440 | tf_op jit(solution)/shard_map/ppermute | solution.py:19
  24.5 28.3 %copy-start = (s32[8,16]{1,0:T(8,128)S(1)}, s32[8,16]{1,0:T(8,128)}, u32[]{:S(2)}) copy-start(s32[8,16]{1,0:T(8,128)} %param.10) | copy-start | bytes 1540
  25.4 26.1 %collective-permute-start.3 = (bf16[8,64,512]{2,1,0:T(8,128)(2,1)}, bf16[8,64,512]{2,1,0:T(8,128)(2,1)S(1)}, u32[]{:S(2)}, u32[]{:S(2)}) collective-permute-start(bf16[8,64,512]{2,1,0:T(8,128)(2,1)} %pad_maximum_fusion.1), channel_id=1, source_target_pairs={{0,16},{2,18},{4,20},{6,22},{8,24},{10,26},{12,28},{14,30},{16,0},... | collective-permute-start | bytes 1572872 | tf_op jit(solution)/shard_map/ppermute | solution.py:19
  28.4 180.4 %reduce-scatter.2.cloned.1.call-start = ((), (), s32[]{:S(2)}) async-start(), calls=%async_computation.2 | async-start | bytes 1572864 | tf_op jit(solution)/shard_map/reduce_scatter | solution.py:69
Sparse Core Ops, SparseCore 0:
  28.6 103.7 all-gather.1
  201.6 7.2 reduce-scatter.1
